TPU v7x, 32 devices: a whole 2x2x4 slice. The times are simulated.
32 devices in a mesh: dp: 8 (over z, x), tensor: 4 (over y, core).
Axes of the slice: x: 2, y: 2, z: 4, core: 2. Of those that a mesh axis runs over, the one named last changes fastest.
Arguments:
- images: bfloat16 [16, 197, 768], P('dp'), may hold values from -6 to 6
- image_counts: int32 [8], P('dp'), may hold values from 1 to 2, as said below
- first_norm_gain: float32 [768], replicated, may hold values from 0.5 to 1.5
- first_norm_bias: float32 [768], replicated, may hold values from -3 to 3
- qkv_weight: bfloat16 [768, 3, 768], P(None, None, 'tensor'), may hold values from -2 to 2
- qv_bias: float32 [2, 768], P(None, 'tensor'), may hold values from -3 to 3
- out_weight: bfloat16 [768, 768], P('tensor'), may hold values from -1.25 to 1.25
- out_bias: float32 [768], replicated, may hold values from -3 to 3
- second_norm_gain: float32 [768], replicated, may hold values from 0.5 to 1.5
- second_norm_bias: float32 [768], replicated, may hold values from -3 to 3
- fc1_weight: bfloat16 [768, 3072], P(None, 'tensor'), may hold values from -0.21875 to 0.21875
- fc1_bias: float32 [3072], P('tensor'), may hold values from -3 to 3
- fc2_weight: bfloat16 [3072, 768], P('tensor'), may hold values from -0.15625 to 0.15625
- fc2_bias: float32 [768], replicated, may hold values from -3 to 3
- cotangent: bfloat16 [16, 197, 768], P('dp'), may hold values from -6 to 6
Outputs:
- block_out: bfloat16 [16, 197, 768], P('dp')
- input_grad: bfloat16 [16, 197, 768], P('dp')
- grad_first_norm_gain: float32 [768], replicated
- grad_first_norm_bias: float32 [768], replicated
- grad_qkv_weight: float32 [768, 3, 768], P(None, None, 'tensor')
- grad_qv_bias: float32 [2, 768], P(None, 'tensor')
- grad_out_weight: float32 [768, 768], P('tensor')
- grad_out_bias: float32 [768], replicated
- grad_second_norm_gain: float32 [768], replicated
- grad_second_norm_bias: float32 [768], replicated
- grad_fc1_weight: float32 [768, 3072], P(None, 'tensor')
- grad_fc1_bias: float32 [3072], P('tensor')
- grad_fc2_weight: float32 [3072, 768], P('tensor')
- grad_fc2_bias: float32 [768], replicated
Inputs may be any that keep to these rules, and one draw needn't show every extreme that they name: `image_counts`: some index of dp has 2 live slots and some has 1; live slots come first in each index's block of 2.
All inputs are finite; a program needn't handle non-finite values.
Results may differ from a plain program's by a relative error of at most 0.02.
Values may be sent and summed in bfloat16 or wider, within the bound.
A program may use at most 128 MiB of HBM per device.

v0:
```python
import jax
import jax.numpy as jnp
from jax import lax
from jax.sharding import PartitionSpec as P

HEAD_DIM = 64
EPS = 1e-06
ROOT_HALF = 0.7071067811865476
INV_ROOT_TAU = 0.3989422804014327


def to_half(array_in):
    return array_in.astype(jnp.bfloat16)


def norm_forward(row_values, gain_vec, shift_vec):
    centre = row_values - jnp.mean(row_values, axis=-1, keepdims=True)
    inverse = lax.rsqrt(jnp.mean(centre * centre, axis=-1, keepdims=True) + EPS)
    scaled = centre * inverse
    return (scaled * gain_vec + shift_vec, scaled, inverse)


def norm_backward(grad_out, scaled, inverse, gain_vec):
    grad_scaled = grad_out * gain_vec
    grad_rows = inverse * (
        grad_scaled
        - jnp.mean(grad_scaled, axis=-1, keepdims=True)
        - scaled * jnp.mean(grad_scaled * scaled, axis=-1, keepdims=True)
    )
    return (grad_rows, jnp.sum(grad_out * scaled, axis=0), jnp.sum(grad_out, axis=0))


def gelu_value(pre_act):
    return 0.5 * pre_act * (1.0 + jax.scipy.special.erf(pre_act * ROOT_HALF))


def gelu_slope(pre_act):
    return (
        0.5 * (1.0 + jax.scipy.special.erf(pre_act * ROOT_HALF))
        + pre_act * jnp.exp(-0.5 * pre_act * pre_act) * INV_ROOT_TAU
    )


def per_device(
    images,
    image_counts,
    first_norm_gain,
    first_norm_bias,
    qkv_weight,
    qv_bias,
    out_weight,
    out_bias,
    second_norm_gain,
    second_norm_bias,
    fc1_weight,
    fc1_bias,
    fc2_weight,
    fc2_bias,
    cotangent,
):
    f32 = jnp.float32
    slot_count, length, model_width = images.shape
    local_width = qkv_weight.shape[2]
    local_heads = local_width // HEAD_DIM
    row_count = slot_count * length
    score_scale = HEAD_DIM ** (-0.5)
    live_slots = (jnp.arange(slot_count, dtype=jnp.int32) < image_counts[0]).astype(f32)
    row_live = jnp.broadcast_to(live_slots[:, None], (slot_count, length)).reshape(row_count, 1)
    head_shape = (slot_count, length, local_heads, HEAD_DIM)
    row_values = images.reshape(row_count, model_width).astype(f32)
    norm_one, scaled_one, inverse_one = norm_forward(row_values, first_norm_gain, first_norm_bias)
    norm_one = to_half(norm_one)
    qkv_flat = qkv_weight.reshape(model_width, 3 * local_width)
    qkv_shift = jnp.stack([qv_bias[0], jnp.zeros_like(qv_bias[0]), qv_bias[1]])
    qkv_rows = to_half(
        jnp.dot(norm_one, qkv_flat, preferred_element_type=f32).reshape(row_count, 3, local_width)
        + qkv_shift
    )
    queries = qkv_rows[:, 0].reshape(head_shape)
    key_heads = qkv_rows[:, 1].reshape(head_shape)
    value_heads = qkv_rows[:, 2].reshape(head_shape)
    scores = (
        jnp.einsum("bqhd,bkhd->bhqk", queries, key_heads, preferred_element_type=f32) * score_scale
    )
    row_peak = jnp.max(scores, axis=-1, keepdims=True)
    log_total = row_peak + jnp.log(jnp.sum(jnp.exp(scores - row_peak), axis=-1, keepdims=True))
    probs_full = jnp.exp(scores - log_total)
    probs_half = to_half(probs_full)
    context = to_half(
        jnp.einsum("bhqk,bkhd->bqhd", probs_half, value_heads, preferred_element_type=f32)
    )
    context_rows = context.reshape(row_count, local_width)
    attn_part = jnp.dot(context_rows, out_weight, preferred_element_type=f32)
    resid_rows = (
        row_values
        + lax.psum(attn_part.astype(jnp.bfloat16), "tensor").astype(jnp.float32)
        + out_bias
    )
    norm_two, scaled_two, inverse_two = norm_forward(resid_rows, second_norm_gain, second_norm_bias)
    norm_two = to_half(norm_two)
    pre_act = jnp.dot(norm_two, fc1_weight, preferred_element_type=f32) + fc1_bias
    act_half = to_half(gelu_value(pre_act))
    mlp_part = jnp.dot(act_half, fc2_weight, preferred_element_type=f32)
    final_rows = (
        resid_rows
        + lax.psum(mlp_part.astype(jnp.bfloat16), "tensor").astype(jnp.float32)
        + fc2_bias
    )
    block_out = to_half(final_rows * row_live).reshape(slot_count, length, model_width)
    inv_images = 1.0 / (slot_count * lax.axis_size("dp"))
    grad_final = cotangent.reshape(row_count, model_width).astype(f32) * row_live
    grad_final_half = to_half(grad_final)
    grad_act = jnp.dot(grad_final_half, fc2_weight.T, preferred_element_type=f32)
    grad_pre = grad_act * gelu_slope(pre_act)
    grad_pre_half = to_half(grad_pre)
    two_part = jnp.dot(grad_pre_half, fc1_weight.T, preferred_element_type=f32)
    grad_norm_two = lax.psum(two_part.astype(jnp.bfloat16), "tensor").astype(jnp.float32)
    back_two, gain_two, shift_two = norm_backward(
        grad_norm_two, scaled_two, inverse_two, second_norm_gain
    )
    mlp_grads = (
        jnp.dot(norm_two.T, grad_pre_half, preferred_element_type=f32) * inv_images,
        jnp.sum(grad_pre, axis=0, keepdims=True) * inv_images,
        jnp.dot(act_half.T, grad_final_half, preferred_element_type=f32) * inv_images,
        jnp.stack([gain_two, shift_two, jnp.sum(grad_final, axis=0)]) * inv_images,
    )
    grad_resid = grad_final + back_two
    grad_resid_half = to_half(grad_resid)
    grad_context = to_half(
        jnp.dot(grad_resid_half, out_weight.T, preferred_element_type=f32)
    ).reshape(head_shape)
    grad_probs = jnp.einsum(
        "bqhd,bkhd->bhqk", grad_context, value_heads, preferred_element_type=f32
    )
    grad_scores = to_half(
        probs_full
        * (grad_probs - jnp.sum(probs_full * grad_probs, axis=-1, keepdims=True))
        * score_scale
    )
    grad_queries = jnp.einsum(
        "bhqk,bkhd->bqhd", grad_scores, key_heads, preferred_element_type=f32
    ).reshape(row_count, local_width)
    grad_keys = jnp.einsum(
        "bhqk,bqhd->bkhd", grad_scores, queries, preferred_element_type=f32
    ).reshape(row_count, local_width)
    grad_values = jnp.einsum(
        "bhqk,bqhd->bkhd", probs_half, grad_context, preferred_element_type=f32
    ).reshape(row_count, local_width)
    grad_qkv_half = to_half(jnp.stack([grad_queries, grad_keys, grad_values], axis=1)).reshape(
        row_count, 3 * local_width
    )
    one_part = jnp.dot(grad_qkv_half, qkv_flat.T, preferred_element_type=f32)
    grad_norm_one = lax.psum(one_part.astype(jnp.bfloat16), "tensor").astype(jnp.float32)
    back_one, gain_one, shift_one = norm_backward(
        grad_norm_one, scaled_one, inverse_one, first_norm_gain
    )
    input_grad = to_half(grad_resid + back_one).reshape(slot_count, length, model_width)
    attn_grads = (
        jnp.dot(norm_one.T, grad_qkv_half, preferred_element_type=f32) * inv_images,
        jnp.stack([jnp.sum(grad_queries, axis=0), jnp.sum(grad_values, axis=0)]) * inv_images,
        jnp.dot(context_rows.T, grad_resid_half, preferred_element_type=f32) * inv_images,
        jnp.stack([gain_one, shift_one, jnp.sum(grad_resid, axis=0)]) * inv_images,
    )
    shares = (
        lax.psum_scatter(attn_grads[0], "dp", scatter_dimension=1, tiled=True),
        lax.psum_scatter(attn_grads[1], "dp", scatter_dimension=1, tiled=True),
        lax.psum_scatter(attn_grads[2], "dp", scatter_dimension=1, tiled=True),
        lax.psum_scatter(attn_grads[3], "dp", scatter_dimension=1, tiled=True),
        lax.psum_scatter(mlp_grads[0], "dp", scatter_dimension=1, tiled=True),
        lax.psum_scatter(mlp_grads[1], "dp", scatter_dimension=1, tiled=True),
        lax.psum_scatter(mlp_grads[2], "dp", scatter_dimension=1, tiled=True),
        lax.psum_scatter(mlp_grads[3], "dp", scatter_dimension=1, tiled=True),
    )
    gathered = (
        lax.all_gather(shares[0].astype(jnp.bfloat16), "dp", axis=1, tiled=True).astype(
            jnp.float32
        ),
        lax.all_gather(shares[1].astype(jnp.bfloat16), "dp", axis=1, tiled=True).astype(
            jnp.float32
        ),
        lax.all_gather(shares[2].astype(jnp.bfloat16), "dp", axis=1, tiled=True).astype(
            jnp.float32
        ),
        lax.all_gather(shares[3].astype(jnp.bfloat16), "dp", axis=1, tiled=True).astype(
            jnp.float32
        ),
        lax.all_gather(shares[4].astype(jnp.bfloat16), "dp", axis=1, tiled=True).astype(
            jnp.float32
        ),
        lax.all_gather(shares[5].astype(jnp.bfloat16), "dp", axis=1, tiled=True).astype(
            jnp.float32
        ),
        lax.all_gather(shares[6].astype(jnp.bfloat16), "dp", axis=1, tiled=True).astype(
            jnp.float32
        ),
        lax.all_gather(shares[7].astype(jnp.bfloat16), "dp", axis=1, tiled=True).astype(
            jnp.float32
        ),
    )
    attn_full = gathered[:4]
    mlp_full = gathered[4:]
    return (
        block_out,
        input_grad,
        attn_full[3][0],
        attn_full[3][1],
        attn_full[0].reshape(model_width, 3, local_width),
        attn_full[1],
        attn_full[2],
        attn_full[3][2],
        mlp_full[3][0],
        mlp_full[3][1],
        mlp_full[0],
        mlp_full[1][0],
        mlp_full[2],
        mlp_full[3][2],
    )


def solution(mesh):
    placed = (
        P("dp", None, None),
        P("dp"),
        P(),
        P(),
        P(None, None, "tensor"),
        P(None, "tensor"),
        P("tensor", None),
        P(),
        P(),
        P(),
        P(None, "tensor"),
        P("tensor"),
        P("tensor", None),
        P(),
        P("dp", None, None),
    )
    return jax.shard_map(
        per_device,
        mesh=mesh,
        in_specs=placed,
        out_specs=(
            P("dp", None, None),
            P("dp", None, None),
            P(),
            P(),
            P(None, None, "tensor"),
            P(None, "tensor"),
            P("tensor", None),
            P(),
            P(),
            P(),
            P(None, "tensor"),
            P("tensor"),
            P("tensor", None),
            P(),
        ),
        check_vma=False,
    )
```

profile of v0, /device:TPU:0, one launch (start us, length us, event | category | flops | bytes accessed | tf_op | source)
XLA Modules:
  0.0 741.2 jit_solution(13153335465204012786)
XLA Ops:
  7.3 1.7 convert_reduce_fusion.2
  12.3 1.8 fusion.12
  19.7 2.2 convolution_convert_fusion.2
  25.3 33.3 %all-reduce.7.cloned.1.call-done = bf16[394,768]{1,0:T(8,128)(2,1)} async-done(((bf16[394,768]{1,0:T(8,128)(2,1)}), bf16[394,768]{1,0:T(8,128)(2,1)}) %all-reduce.7.cloned.1.call-update) | async-done | bytes 605200 | tf_op jit(solution)/shard_map/psum | solution.py:96
  58.6 1.7 fusion.67
  61.0 1.7 multiply_convert_fusion.1
  62.7 1.5 fusion.76
  65.0 1.5 convolution_convert_fusion
  66.8 2.9 convolution_convert_fusion.1
  69.7 31.1 %all-reduce.9.cloned.1.call-done = bf16[394,768]{1,0:T(8,128)(2,1)} async-done(((bf16[394,768]{1,0:T(8,128)(2,1)}), bf16[394,768]{1,0:T(8,128)(2,1)}) %all-reduce.9.cloned.1.call-update) | async-done | bytes 605200 | tf_op jit(solution)/shard_map/psum | solution.py:117
  100.8 1.8 fusion.26
  106.4 1.4 fusion.50
  107.8 4.5 fusion.69
  112.3 3.8 fusion.34
  116.1 1.7 fusion.70
  118.9 1.6 constant_dynamic-update-slice_fusion.2
  120.5 1.8 copy.151
  126.7 2.9 fusion.10
  130.3 3.4 convolution_multiply_fusion.1
  137.3 3.6 convolution_multiply_fusion
  142.0 26.2 %all-reduce.11.cloned.1.call-done = (bf16[394,768]{1,0:T(8,128)(2,1)}, bf16[394,768]{1,0:T(8,128)(2,1)}) async-done(((bf16[394,768]{1,0:T(8,128)(2,1)}, bf16[394,768]{1,0:T(8,128)(2,1)}), (bf16[394,768]{1,0:T(8,128)(2,1)}, bf16[394,768]{1,0:T(8,128)(2,1)})) %all-reduce.11.cloned.1.call-update) | async-done | bytes 1210384 | tf_op jit(solution)/shard_map/psum | solution.py:106
  168.2 2.1 fusion.27
  171.4 2.4 convolution_multiply_fusion.5
  173.9 2.3 copy.172
  177.2 3.1 convolution_multiply_fusion.2
  180.4 61.4 %reduce-scatter.19.cloned.1.call-done = f32[768,96]{0,1:T(8,128)} async-done(((f32[768,768]{0,1:T(8,128)}), f32[768,96]{0,1:T(8,128)}) %reduce-scatter.19.cloned.1.call-update) | async-done | bytes 294928 | tf_op jit(solution)/shard_map/reduce_scatter | solution.py:169
  241.7 1.6 convert_element_type.193
  245.3 60.9 %reduce-scatter.29.cloned.1.call-done = f32[96,1]{1,0:T(8,128)} async-done(((f32[768,1]{1,0:T(8,128)}), f32[96,1]{1,0:T(8,128)}) %reduce-scatter.29.cloned.1.call-update) | async-done | bytes 400
  307.3 19.5 %all-reduce = bf16[768]{0:T(1024)(128)(2,1)S(1)} all-reduce(bf16[768]{0:T(1024)(128)(2,1)S(1)} %dynamic-update-slice), channel_id=1, replica_groups=mesh['dp'=8,'tensor'=4] {'dp'}, use_global_device_ids=true, to_apply=%add | all-reduce | flops 768 | bytes 3072
  327.6 17.2 %all-reduce.1 = bf16[2,192]{1,0:T(2,128)(2,1)S(1)} all-reduce(f32[2,192]{1,0:T(2,128)S(1)} %maximum_multiply_fusion.2), channel_id=4, replica_groups=mesh['dp'=8,'tensor'=4] {'dp'}, use_global_device_ids=true, to_apply=%region_22.0.clone | all-reduce | flops 384 | bytes 2304
  344.8 18.3 %all-gather.1 = bf16[8,24,2]{1,2,0:T(2,128)(2,1)S(1)} all-gather(bf16[1,24,2]{1,2,0:T(2,128)(2,1)S(1)} %fusion.60), channel_id=1, replica_groups=mesh['dp'=8,'tensor'=4] {'dp'}, dimensions={0}, use_global_device_ids=true | all-gather | bytes 864 | tf_op jit(solution)/shard_map/all_gather | solution.py:178
  363.8 7.4 %reduce-scatter.27.cloned.1.call-done = f32[96,3]{1,0:T(8,128)} async-done(((f32[768,3]{1,0:T(8,128)}), f32[96,3]{1,0:T(8,128)}) %reduce-scatter.27.cloned.1.call-update) | async-done | bytes 1168
  372.1 19.0 %all-gather.2 = bf16[8,96,3]{1,2,0:T(4,128)(2,1)S(1)} all-gather(bf16[1,96,3]{1,2,0:T(4,128)(2,1)S(1)} %bitcast.107), channel_id=1, replica_groups=mesh['dp'=8,'tensor'=4] {'dp'}, dimensions={0}, use_global_device_ids=true | all-gather | bytes 5184 | tf_op jit(solution)/shard_map/all_gather | solution.py:196
  391.1 52.8 %reduce-scatter.21.cloned.1.call-done = f32[768,96]{0,1:T(8,128)} async-done(((f32[768,768]{0,1:T(8,128)}), f32[768,96]{0,1:T(8,128)}) %reduce-scatter.21.cloned.1.call-update) | async-done | bytes 294928 | tf_op jit(solution)/shard_map/reduce_scatter | solution.py:171
  443.9 1.6 convert_element_type.196
  446.3 2.2 multiply_convert_fusion
  448.5 2.1 reshape.214
  450.6 2.5 copy.159
  456.9 51.7 %reduce-scatter.23.cloned.1.call-done = f32[96,3]{1,0:T(8,128)} async-done(((f32[768,3]{1,0:T(8,128)}), f32[96,3]{1,0:T(8,128)}) %reduce-scatter.23.cloned.1.call-update) | async-done | bytes 1168
  509.4 18.7 %all-gather = bf16[8,96,3]{1,2,0:T(4,128)(2,1)S(1)} all-gather(bf16[1,96,3]{1,2,0:T(4,128)(2,1)S(1)} %bitcast.108), channel_id=1, replica_groups=mesh['dp'=8,'tensor'=4] {'dp'}, dimensions={0}, use_global_device_ids=true | all-gather | bytes 5184 | tf_op jit(solution)/shard_map/all_gather | solution.py:184
  528.8 45.3 %reduce-scatter.25.cloned.1.call-done = f32[96,192]{1,0:T(8,128)} async-done(((f32[768,192]{1,0:T(8,128)}), f32[96,192]{1,0:T(8,128)}) %reduce-scatter.25.cloned.1.call-update) | async-done | bytes 73744
  575.2 31.8 %all_gather.27 = bf16[192,768]{0,1:T(8,128)(2,1)S(1)} all-gather(bf16[192,96]{0,1:T(8,128)(2,1)S(1)} %copy.157), channel_id=1, replica_groups=mesh['dp'=8,'tensor'=4] {'dp'}, dimensions={1}, use_global_device_ids=true | all-gather | bytes 331776 | tf_op jit(solution)/shard_map/all_gather | solution.py:181
  608.0 36.5 %reduce-scatter.17.cloned.1.call-done = f32[768,72]{0,1:T(8,128)} async-done(((f32[768,576]{0,1:T(8,128)}), f32[768,72]{0,1:T(8,128)}) %reduce-scatter.17.cloned.1.call-update) | async-done | bytes 221200 | tf_op jit(solution)/shard_map/reduce_scatter | solution.py:165
  645.4 33.5 %all_gather.25 = bf16[768,576]{0,1:T(8,128)(2,1)S(1)} all-gather(bf16[768,72]{0,1:T(8,128)(2,1)S(1)} %convert_element_type.185), channel_id=1, replica_groups=mesh['dp'=8,'tensor'=4] {'dp'}, dimensions={1}, use_global_device_ids=true | all-gather | bytes 995328 | tf_op jit(solution)/shard_map/all_gather | solution.py:175
  680.3 8.9 %all-gather.6.cloned.1.call-done = bf16[768,768]{0,1:T(8,128)(2,1)} async-done(((bf16[768,96]{0,1:T(8,128)(2,1)}), bf16[768,768]{0,1:T(8,128)(2,1)}) %all-gather.6.cloned.1.call-update) | async-done | bytes 1179664 | tf_op jit(solution)/shard_map/all_gather | solution.py:187
  689.1 2.7 copy.162
  691.9 39.8 %all-gather.8.cloned.1.call-done = bf16[768,768]{0,1:T(8,128)(2,1)} async-done(((bf16[768,96]{0,1:T(8,128)(2,1)}), bf16[768,768]{0,1:T(8,128)(2,1)}) %all-gather.8.cloned.1.call-update) | async-done | bytes 1179664 | tf_op jit(solution)/shard_map/all_gather | solution.py:193
  731.6 2.7 copy.163
  (188 shorter events, 44.3 us)
Async XLA Ops:
  7.2 53.4 %copy-start = (bf16[768,768]{1,0:T(8,128)(2,1)S(1)}, bf16[768,768]{1,0:T(8,128)(2,1)}, u32[]{:S(2)}) copy-start(bf16[768,768]{1,0:T(8,128)(2,1)} %param.25) | copy-start | bytes 3538948
  7.2 1.8 copy-start.7
  7.2 3.0 copy-start.24
  7.2 3.0 copy-start.22
  7.2 51.3 %all-reduce.7.cloned.1.call-start = ((), (), s32[]{:S(2)}) async-start(), calls=%async_computation.7 | async-start | bytes 1228800 | tf_op jit(solution)/shard_map/psum | solution.py:96
  10.2 1.3 copy-start.16
  11.6 2.6 copy-start.8
  14.5 2.4 copy-start.18
  16.7 1.0 copy-start.1
  19.6 2.3 copy-start.13
  21.9 78.9 %all-reduce.9.cloned.1.call-start = ((), (), s32[]{:S(2)}) async-start(), calls=%async_computation.8 | async-start | bytes 1228800 | tf_op jit(solution)/shard_map/psum | solution.py:117
  22.1 1.2 copy-start.12
  23.3 35.3 %copy-start.25 = (f32[768]{0:T(1024)S(1)}, f32[768]{0:T(1024)}, u32[]{:S(2)}) copy-start(f32[768]{0:T(1024)} %param.22) | copy-start | bytes 9220
  25.1 35.1 %copy-start.31 = (f32[2]{0:T(128)}, f32[2]{0:T(128)S(1)}, u32[]{:S(2)}) copy-start(f32[2]{0:T(128)S(1)} %compare_convert_fusion) | copy-start | bytes 28
  60.3 0.7 copy-start.23
  60.3 0.7 copy-start.34
  60.3 0.7 copy-start.35
  61.0 1.7 copy-start.5
  61.0 1.7 copy-start.33
  64.2 0.8 copy-start.37
  66.5 101.7 %all-reduce.11.cloned.1.call-start = ((), (), s32[]{:S(2)}) async-start(), calls=%async_computation.18 | async-start | bytes 2457600 | tf_op jit(solution)/shard_map/psum | solution.py:106
  100.8 1.9 copy-start.6
  100.8 1.9 copy-start.11
  102.7 1.6 copy-start.15
  103.2 1.1 copy-start.3
  107.8 4.5 copy-start.19
  116.1 1.7 copy-start.21
  129.6 0.7 copy-start.36
  129.6 112.1 %reduce-scatter.19.cloned.1.call-start = ((), (), s32[]{:S(2)}) async-start(), calls=%async_computation.10 | async-start | bytes 2654208 | tf_op jit(solution)/shard_map/reduce_scatter | solution.py:169
  133.7 1.5 copy-start.27
  133.7 172.5 %reduce-scatter.29.cloned.1.call-start = ((), (), s32[]{:S(2)}) async-start(), calls=%async_computation.17 | async-start | bytes 442368
  135.2 2.1 copy-start.20
  136.2 235.0 %reduce-scatter.27.cloned.1.call-start = ((), (), s32[]{:S(2)}) async-start(), calls=%async_computation.16 | async-start | bytes 442368
  137.2 306.7 %reduce-scatter.21.cloned.1.call-start = ((), (), s32[]{:S(2)}) async-start(), calls=%async_computation.12 | async-start | bytes 2654208 | tf_op jit(solution)/shard_map/reduce_scatter | solution.py:171
  140.9 0.9 copy-start.17
  140.9 367.6 %reduce-scatter.23.cloned.1.call-start = ((), (), s32[]{:S(2)}) async-start(), calls=%async_computation.14 | async-start | bytes 442368
  168.2 3.2 copy-start.14
  171.4 402.7 %reduce-scatter.25.cloned.1.call-start = ((), (), s32[]{:S(2)}) async-start(), calls=%async_computation.15 | async-start | bytes 884736
  173.9 2.4 copy-start.9
  176.2 468.3 %reduce-scatter.17.cloned.1.call-start = ((), (), s32[]{:S(2)}) async-start(), calls=%async_computation.9 | async-start | bytes 1990656 | tf_op jit(solution)/shard_map/reduce_scatter | solution.py:165
  180.3 63.2 %copy-start.28 = (u32[32]{0:T(128)S(1)}, u32[32]{0:T(128)}, u32[]{:S(2)}) copy-start(u32[32]{0:T(128)} %constant.41) | copy-start | bytes 388
  180.3 147.2 %copy-start.29 = (f32[3,64]{1,0:T(4,128)S(1)}, f32[3,64]{1,0:T(4,128)}, u32[]{:S(2)}) copy-start(f32[3,64]{1,0:T(4,128)} %get-tuple-element.107) | copy-start | bytes 2308
  180.3 266.0 %copy-start.26 = (f32[768]{0:T(1024)S(1)}, f32[768]{0:T(1024)}, u32[]{:S(2)}) copy-start(f32[768]{0:T(1024)} %param.28) | copy-start | bytes 9220
  180.3 508.8 %all-gather.6.cloned.1.call-start = ((), (), s32[]{:S(2)}) async-start(), calls=%async_computation.11 | async-start | bytes 1327104 | tf_op jit(solution)/shard_map/all_gather | solution.py:187
  243.4 488.2 %all-gather.8.cloned.1.call-start = ((), (), s32[]{:S(2)}) async-start(), calls=%async_computation.13 | async-start | bytes 1327104 | tf_op jit(solution)/shard_map/all_gather | solution.py:193
  446.3 6.7 copy-start.10
  448.5 4.6 copy-start.2
  450.6 2.5 copy-start.4
  (2 other events, 1.3 us)
Sparse Core Ops, SparseCore 0:
  22.0 36.4 all-reduce.6
  66.6 34.0 all-reduce.8
  129.7 38.4 all-reduce.10
  172.1 69.5 reduce-scatter.18
  244.8 61.3 reduce-scatter.28
  309.9 61.2 reduce-scatter.26
  375.3 68.6 reduce-scatter.20
  447.2 61.3 reduce-scatter.22
  511.9 62.2 reduce-scatter.24
  578.0 66.4 reduce-scatter.16
  646.7 42.4 all-gather.5
  691.2 40.3 all-gather.7
where the time goes:
time: 743 us; the launch traced here: 741 us
  waiting for transfers between devices  455 us (61%)
  blocking collectives  158 us (21%)
  local copies, waits for them, and re-layouts  47.1 us (6%)
  matrix products  41.1 us (6%)
  other arithmetic  22.2 us (3%)
  between operations  16.8 us (2%)
    unnamed x16, waiting for transfers between devices  166 us
    reduce_scatter x1, waiting for transfers between devices, per_device(): lax.psum_scatter(mlp_grads[0], 'dp', scatter_dimension=1, tiled=True)  61.4 us
    reduce_scatter x1, waiting for transfers between devices, per_device(): lax.psum_scatter(mlp_grads[2], 'dp', scatter_dimension=1, tiled=True)  52.8 us
    all_gather x1, waiting for transfers between devices, per_device(): lax.all_gather(shares[6].astype(jnp.bfloat16), 'dp', axis=1, tiled=True)  39.8 us
    unnamed x2, blocking collectives  36.6 us
    reduce_scatter x1, waiting for transfers between devices, per_device(): lax.psum_scatter(attn_grads[0], 'dp', scatter_dimension=1, tiled=True)  36.5 us
    all_gather x1, blocking collectives, per_device(): lax.all_gather(shares[0].astype(jnp.bfloat16), 'dp', axis=1, tiled=True)  33.5 us
    psum x1, waiting for transfers between devices, per_device(): lax.psum(attn_part.astype(jnp.bfloat16), 'tensor').astype(jnp.float32)  33.3 us
  transfers between devices with their start and end apart: 12, of which 12 were waited for; matrix products, arithmetic and copies ran while one was open for 7% of the time, Pallas kernels for 0%

commit v1 on v0

--- a/solution.py
+++ b/solution.py
@@ -171,6 +171,21 @@
         lax.psum_scatter(mlp_grads[2], "dp", scatter_dimension=1, tiled=True),
         lax.psum_scatter(mlp_grads[3], "dp", scatter_dimension=1, tiled=True),
     )
+
+    def divide_ladders(content):
+        main = lax.psum(1, axis_name="dp")
+        mid_arr = lax.axis_index("dp")
+        finding, u_next, last = (main, mid_arr, content.shape[1])
+        far_arr, tmp = (content, 1)
+        while tmp < finding:
+            known = lax.ppermute(
+                far_arr, axis_name="dp", perm=[(jj, (jj - tmp) % finding) for jj in range(finding)]
+            )
+            far_arr = jnp.concatenate([far_arr, known], axis=1)
+            tmp = 2 * tmp
+        local_part = jnp.roll(far_arr, u_next * last, axis=1)
+        return local_part
+
     gathered = (
         lax.all_gather(shares[0].astype(jnp.bfloat16), "dp", axis=1, tiled=True).astype(
             jnp.float32
@@ -190,9 +205,7 @@
         lax.all_gather(shares[5].astype(jnp.bfloat16), "dp", axis=1, tiled=True).astype(
             jnp.float32
         ),
-        lax.all_gather(shares[6].astype(jnp.bfloat16), "dp", axis=1, tiled=True).astype(
-            jnp.float32
-        ),
+        divide_ladders(shares[6].astype(jnp.bfloat16)).astype(jnp.float32),
         lax.all_gather(shares[7].astype(jnp.bfloat16), "dp", axis=1, tiled=True).astype(
             jnp.float32
         ),

time: 743 us -> 720 us (0.969)
  waiting for transfers between devices: 455 us -> 407 us
  blocking collectives: 158 us -> 180 us
    all_gather x1 -> x0, waiting for transfers between devices: 39.8 us -> none  [per_device(): lax.all_gather(shares[6].astype(jnp.bfloat16), 'dp', axis=1, tiled=True)]
    all_gather x1, blocking collectives: 33.5 us -> 55.4 us  [per_device(): lax.all_gather(shares[0].astype(jnp.bfloat16), 'dp', axis=1, tiled=True)]
    all_gather x1, waiting for transfers between devices: 8.89 us -> 0.01 us  [per_device(): lax.all_gather(shares[4].astype(jnp.bfloat16), 'dp', axis=1, tiled=True)]
    reduce_scatter x1, waiting for transfers between devices: 61.4 us -> 53 us  [per_device(): lax.psum_scatter(mlp_grads[0], 'dp', scatter_dimension=1, tiled=True)]
    unnamed x16 -> x15, waiting for transfers between devices: 166 us -> 173 us
    unnamed x97 -> x105, local copies, waits for them, and re-layouts: 26.6 us -> 27.6 us
  transfers between devices with their start and end apart: 12 -> 14, of which waited for: 12 -> 10; matrix products, arithmetic and copies ran while one was open for 7% -> 7% of each run, Pallas kernels for 0% -> 0%
where the time goes in v1:
time: 720 us; the launch traced here: 719 us
  waiting for transfers between devices  407 us (57%)
  blocking collectives  180 us (25%)
  local copies, waits for them, and re-layouts  45 us (6%)
  matrix products  40.1 us (6%)
  other arithmetic  24.8 us (3%)
  between operations  16.6 us (2%)
    unnamed x15, waiting for transfers between devices  173 us
    all_gather x1, blocking collectives, per_device(): lax.all_gather(shares[0].astype(jnp.bfloat16), 'dp', axis=1, tiled=True)  55.4 us
    reduce_scatter x1, waiting for transfers between devices, per_device(): lax.psum_scatter(mlp_grads[0], 'dp', scatter_dimension=1, tiled=True)  53 us
    reduce_scatter x1, waiting for transfers between devices, per_device(): lax.psum_scatter(mlp_grads[2], 'dp', scatter_dimension=1, tiled=True)  49.1 us
    unnamed x2, blocking collectives  36.6 us
    reduce_scatter x1, waiting for transfers between devices, per_device(): lax.psum_scatter(attn_grads[0], 'dp', scatter_dimension=1, tiled=True)  36.4 us
    psum x1, waiting for transfers between devices, per_device(): lax.psum(attn_part.astype(jnp.bfloat16), 'tensor').astype(jnp.float32)  33.3 us
    all_gather x1, blocking collectives, per_device(): lax.all_gather(shares[2].astype(jnp.bfloat16), 'dp', axis=1, tiled=True)  31.5 us
  transfers between devices with their start and end apart: 14, of which 10 were waited for; matrix products, arithmetic and copies ran while one was open for 7% of the time, Pallas kernels for 0%

profile of v1, /device:TPU:0, one launch (start us, length us, event | category | flops | bytes accessed | tf_op | source)
XLA Modules:
  0.0 718.7 jit_solution(4626761691306035626)
XLA Ops:
  7.3 1.7 convert_reduce_fusion.2
  12.3 1.8 fusion.12
  19.7 2.2 convolution_convert_fusion.2
  25.3 33.3 %all-reduce.7.cloned.1.call-done = bf16[394,768]{1,0:T(8,128)(2,1)} async-done(((bf16[394,768]{1,0:T(8,128)(2,1)}), bf16[394,768]{1,0:T(8,128)(2,1)}) %all-reduce.7.cloned.1.call-update) | async-done | bytes 605200 | tf_op jit(solution)/shard_map/psum | solution.py:96
  58.6 1.7 fusion.67
  61.0 1.7 multiply_convert_fusion.1
  62.7 1.5 fusion.76
  65.0 1.5 convolution_convert_fusion
  66.8 2.9 convolution_convert_fusion.1
  69.7 31.1 %all-reduce.9.cloned.1.call-done = bf16[394,768]{1,0:T(8,128)(2,1)} async-done(((bf16[394,768]{1,0:T(8,128)(2,1)}), bf16[394,768]{1,0:T(8,128)(2,1)}) %all-reduce.9.cloned.1.call-update) | async-done | bytes 605200 | tf_op jit(solution)/shard_map/psum | solution.py:117
  100.8 1.8 fusion.26
  106.4 1.4 fusion.50
  107.8 4.5 fusion.69
  112.3 3.8 fusion.34
  116.1 1.7 fusion.70
  118.9 1.6 constant_dynamic-update-slice_fusion.2
  120.5 1.8 copy.151
  126.7 2.9 fusion.10
  133.2 3.6 convolution_multiply_fusion
  137.9 30.3 %all-reduce.11.cloned.1.call-done = (bf16[394,768]{1,0:T(8,128)(2,1)}, bf16[394,768]{1,0:T(8,128)(2,1)}) async-done(((bf16[394,768]{1,0:T(8,128)(2,1)}, bf16[394,768]{1,0:T(8,128)(2,1)}), (bf16[394,768]{1,0:T(8,128)(2,1)}, bf16[394,768]{1,0:T(8,128)(2,1)})) %all-reduce.11.cloned.1.call-update) | async-done | bytes 1210384 | tf_op jit(solution)/shard_map/psum | solution.py:106
  168.3 2.2 fusion.27
  171.5 2.4 convolution_multiply_fusion.1
  174.8 2.4 convolution_multiply_fusion.5
  177.2 2.3 copy.172
  180.6 3.1 convolution_multiply_fusion.2
  186.2 47.5 %reduce-scatter.29.cloned.1.call-done = f32[96,1]{1,0:T(8,128)} async-done(((f32[768,1]{1,0:T(8,128)}), f32[96,1]{1,0:T(8,128)}) %reduce-scatter.29.cloned.1.call-update) | async-done | bytes 400
  234.8 19.5 %all-reduce = bf16[768]{0:T(1024)(128)(2,1)S(1)} all-reduce(bf16[768]{0:T(1024)(128)(2,1)S(1)} %dynamic-update-slice), channel_id=1, replica_groups=mesh['dp'=8,'tensor'=4] {'dp'}, use_global_device_ids=true, to_apply=%add | all-reduce | flops 768 | bytes 3072
  255.0 17.1 %all-reduce.1 = bf16[2,192]{1,0:T(2,128)(2,1)S(1)} all-reduce(f32[2,192]{1,0:T(2,128)S(1)} %maximum_multiply_fusion.2), channel_id=4, replica_groups=mesh['dp'=8,'tensor'=4] {'dp'}, use_global_device_ids=true, to_apply=%region_22.0.clone | all-reduce | flops 384 | bytes 2304
  272.2 18.3 %all-gather.1 = bf16[8,24,2]{1,2,0:T(2,128)(2,1)S(1)} all-gather(bf16[1,24,2]{1,2,0:T(2,128)(2,1)S(1)} %fusion.60), channel_id=1, replica_groups=mesh['dp'=8,'tensor'=4] {'dp'}, dimensions={0}, use_global_device_ids=true | all-gather | bytes 864 | tf_op jit(solution)/shard_map/all_gather | solution.py:193
  291.2 7.5 %reduce-scatter.27.cloned.1.call-done = f32[96,3]{1,0:T(8,128)} async-done(((f32[768,3]{1,0:T(8,128)}), f32[96,3]{1,0:T(8,128)}) %reduce-scatter.27.cloned.1.call-update) | async-done | bytes 1168
  299.6 19.0 %all-gather.2 = bf16[8,96,3]{1,2,0:T(4,128)(2,1)S(1)} all-gather(bf16[1,96,3]{1,2,0:T(4,128)(2,1)S(1)} %bitcast.107), channel_id=1, replica_groups=mesh['dp'=8,'tensor'=4] {'dp'}, dimensions={0}, use_global_device_ids=true | all-gather | bytes 5184 | tf_op jit(solution)/shard_map/all_gather | solution.py:209
  319.3 3.0 fusion.16
  322.3 49.1 %reduce-scatter.21.cloned.1.call-done = f32[768,96]{0,1:T(8,128)} async-done(((f32[768,768]{0,1:T(8,128)}), f32[768,96]{0,1:T(8,128)}) %reduce-scatter.21.cloned.1.call-update) | async-done | bytes 294928 | tf_op jit(solution)/shard_map/reduce_scatter | solution.py:171
  371.4 1.6 constant_dynamic-update-slice_fusion.10
  373.1 2.1 collective-permute-start
  379.3 56.8 %reduce-scatter.23.cloned.1.call-done = f32[96,3]{1,0:T(8,128)} async-done(((f32[768,3]{1,0:T(8,128)}), f32[96,3]{1,0:T(8,128)}) %reduce-scatter.23.cloned.1.call-update) | async-done | bytes 1168
  436.9 18.8 %all-gather = bf16[8,96,3]{1,2,0:T(4,128)(2,1)S(1)} all-gather(bf16[1,96,3]{1,2,0:T(4,128)(2,1)S(1)} %bitcast.108), channel_id=1, replica_groups=mesh['dp'=8,'tensor'=4] {'dp'}, dimensions={0}, use_global_device_ids=true | all-gather | bytes 5184 | tf_op jit(solution)/shard_map/all_gather | solution.py:199
  455.8 53.0 %reduce-scatter.19.cloned.1.call-done = f32[768,96]{0,1:T(8,128)} async-done(((f32[768,768]{0,1:T(8,128)}), f32[768,96]{0,1:T(8,128)}) %reduce-scatter.19.cloned.1.call-update) | async-done | bytes 294928 | tf_op jit(solution)/shard_map/reduce_scatter | solution.py:169
  508.7 1.6 convert_element_type.193
  510.4 2.0 collective-permute-start.1
  513.2 61.4 %reduce-scatter.25.cloned.1.call-done = f32[96,192]{1,0:T(8,128)} async-done(((f32[768,192]{1,0:T(8,128)}), f32[96,192]{1,0:T(8,128)}) %reduce-scatter.25.cloned.1.call-update) | async-done | bytes 73744
  575.7 31.5 %all_gather.24 = bf16[192,768]{0,1:T(8,128)(2,1)S(1)} all-gather(bf16[192,96]{0,1:T(8,128)(2,1)S(1)} %copy.157), channel_id=1, replica_groups=mesh['dp'=8,'tensor'=4] {'dp'}, dimensions={1}, use_global_device_ids=true | all-gather | bytes 331776 | tf_op jit(solution)/shard_map/all_gather | solution.py:196
  608.2 36.4 %reduce-scatter.17.cloned.1.call-done = f32[768,72]{0,1:T(8,128)} async-done(((f32[768,576]{0,1:T(8,128)}), f32[768,72]{0,1:T(8,128)}) %reduce-scatter.17.cloned.1.call-update) | async-done | bytes 221200 | tf_op jit(solution)/shard_map/reduce_scatter | solution.py:165
  646.8 55.4 %all_gather.22 = bf16[768,576]{0,1:T(8,128)(2,1)S(1)} all-gather(bf16[768,72]{0,1:T(8,128)(2,1)S(1)} %convert_element_type.185), channel_id=1, replica_groups=mesh['dp'=8,'tensor'=4] {'dp'}, dimensions={1}, use_global_device_ids=true | all-gather | bytes 995328 | tf_op jit(solution)/shard_map/all_gather | solution.py:190
  702.2 1.4 convert.20
  704.8 1.6 dynamic-slice_convert_fusion
  706.4 3.0 copy.163
  709.5 2.7 copy.162
  (203 shorter events, 46.4 us)
Async XLA Ops:
  7.2 53.4 %copy-start = (bf16[768,768]{1,0:T(8,128)(2,1)S(1)}, bf16[768,768]{1,0:T(8,128)(2,1)}, u32[]{:S(2)}) copy-start(bf16[768,768]{1,0:T(8,128)(2,1)} %param.25) | copy-start | bytes 3538948
  7.2 1.8 copy-start.5
  7.2 3.0 copy-start.24
  7.2 3.0 copy-start.22
  7.2 51.3 %all-reduce.7.cloned.1.call-start = ((), (), s32[]{:S(2)}) async-start(), calls=%async_computation.7 | async-start | bytes 1228800 | tf_op jit(solution)/shard_map/psum | solution.py:96
  10.2 1.3 copy-start.15
  11.6 2.6 copy-start.6
  14.5 2.4 copy-start.17
  16.7 1.0 copy-start.1
  19.6 2.3 copy-start.12
  21.9 78.9 %all-reduce.9.cloned.1.call-start = ((), (), s32[]{:S(2)}) async-start(), calls=%async_computation.8 | async-start | bytes 1228800 | tf_op jit(solution)/shard_map/psum | solution.py:117
  22.1 1.2 copy-start.11
  23.3 35.3 %copy-start.25 = (f32[768]{0:T(1024)S(1)}, f32[768]{0:T(1024)}, u32[]{:S(2)}) copy-start(f32[768]{0:T(1024)} %param.22) | copy-start | bytes 9220
  25.1 35.1 %copy-start.31 = (f32[2]{0:T(128)}, f32[2]{0:T(128)S(1)}, u32[]{:S(2)}) copy-start(f32[2]{0:T(128)S(1)} %compare_convert_fusion) | copy-start | bytes 28
  60.3 0.7 copy-start.35
  61.0 1.7 copy-start.3
  61.0 1.7 copy-start.33
  64.2 0.8 copy-start.37
  66.5 101.7 %all-reduce.11.cloned.1.call-start = ((), (), s32[]{:S(2)}) async-start(), calls=%async_computation.17 | async-start | bytes 2457600 | tf_op jit(solution)/shard_map/psum | solution.py:106
  100.8 1.9 copy-start.4
  100.8 1.9 copy-start.10
  102.7 1.6 copy-start.14
  103.2 1.1 copy-start.2
  107.8 4.5 copy-start.18
  116.1 1.7 copy-start.21
  129.6 1.5 copy-start.27
  129.6 104.0 %reduce-scatter.29.cloned.1.call-start = ((), (), s32[]{:S(2)}) async-start(), calls=%async_computation.16 | async-start | bytes 442368
  131.1 2.1 copy-start.20
  132.1 166.6 %reduce-scatter.27.cloned.1.call-start = ((), (), s32[]{:S(2)}) async-start(), calls=%async_computation.15 | async-start | bytes 442368
  133.1 238.3 %reduce-scatter.21.cloned.1.call-start = ((), (), s32[]{:S(2)}) async-start(), calls=%async_computation.12 | async-start | bytes 2654208 | tf_op jit(solution)/shard_map/reduce_scatter | solution.py:171
  136.8 0.9 copy-start.16
  136.8 299.3 %reduce-scatter.23.cloned.1.call-start = ((), (), s32[]{:S(2)}) async-start(), calls=%async_computation.13 | async-start | bytes 442368
  168.2 3.2 copy-start.36
  168.2 3.3 copy-start.38
  171.4 337.3 %reduce-scatter.19.cloned.1.call-start = ((), (), s32[]{:S(2)}) async-start(), calls=%async_computation.10 | async-start | bytes 2654208 | tf_op jit(solution)/shard_map/reduce_scatter | solution.py:169
  173.9 0.9 copy-start.13
  173.9 400.7 %reduce-scatter.25.cloned.1.call-start = ((), (), s32[]{:S(2)}) async-start(), calls=%async_computation.14 | async-start | bytes 884736
  177.2 2.4 copy-start.7
  179.5 465.0 %reduce-scatter.17.cloned.1.call-start = ((), (), s32[]{:S(2)}) async-start(), calls=%async_computation.9 | async-start | bytes 1990656 | tf_op jit(solution)/shard_map/reduce_scatter | solution.py:165
  183.6 71.3 %copy-start.29 = (f32[3,64]{1,0:T(4,128)S(1)}, f32[3,64]{1,0:T(4,128)}, u32[]{:S(2)}) copy-start(f32[3,64]{1,0:T(4,128)} %get-tuple-element.109) | copy-start | bytes 2308
  183.6 135.6 %copy-start.8 = (bf16[394,768]{1,0:T(8,128)(2,1)S(1)}, bf16[394,768]{1,0:T(8,128)(2,1)}, u32[]{:S(2)}) copy-start(bf16[394,768]{1,0:T(8,128)(2,1)} %get-tuple-element.99) | copy-start | bytes 1815556
  183.7 525.8 %all-gather.5.cloned.1.call-start = ((), (), s32[]{:S(2)}) async-start(), calls=%async_computation.11 | async-start | bytes 1327104 | tf_op jit(solution)/shard_map/all_gather | solution.py:202
  319.3 55.9 %copy-start.26 = (f32[768]{0:T(1024)S(1)}, f32[768]{0:T(1024)}, u32[]{:S(2)}) copy-start(f32[768]{0:T(1024)} %param.28) | copy-start | bytes 9220
  373.1 137.3 %collective-permute-start = (bf16[768,96]{0,1:T(8,128)(2,1)S(1)}, bf16[768,96]{0,1:T(8,128)(2,1)S(1)}, u32[]{:S(2)}, u32[]{:S(2)}) collective-permute-start(bf16[768,96]{0,1:T(8,128)(2,1)S(1)} %get-tuple-element.101), channel_id=1, source_target_pairs={{0,28},{4,0},{8,4},{12,8},{16,12},{20,16},{24,20},{28,24},{1,29},{... | collective-permute-start | bytes 442376 | tf_op jit(solution)/shard_map/ppermute | solution.py:181
  376.4 1.4 copy-start.9
  510.4 135.1 %collective-permute-start.1 = (bf16[768,192]{0,1:T(8,128)(2,1)S(1)}, bf16[768,192]{0,1:T(8,128)(2,1)S(1)}, u32[]{:S(2)}, u32[]{:S(2)}) collective-permute-start(bf16[768,192]{0,1:T(8,128)(2,1)S(1)} %pad_maximum_fusion.1), channel_id=1, source_target_pairs={{0,24},{4,28},{8,0},{12,4},{16,8},{20,12},{24,16},{28,20},{1,25},{... | collective-permute-start | bytes 884744 | tf_op jit(solution)/shard_map/ppermute | solution.py:181
  645.6 59.0 %collective-permute-start.2 = (bf16[768,384]{0,1:T(8,128)(2,1)S(1)}, bf16[768,384]{0,1:T(8,128)(2,1)S(1)}, u32[]{:S(2)}, u32[]{:S(2)}) collective-permute-start(bf16[768,384]{0,1:T(8,128)(2,1)S(1)} %pad_maximum_fusion), channel_id=1, source_target_pairs={{0,16},{4,20},{8,24},{12,28},{16,0},{20,4},{24,8},{28,12},{1,17},{... | collective-permute-start | bytes 1769480 | tf_op jit(solution)/shard_map/ppermute | solution.py:181
  702.2 2.3 copy-start.19
  (5 other events, 3.4 us)
Sparse Core Ops, SparseCore 0:
  22.0 36.4 all-reduce.6
  66.7 34.0 all-reduce.8
  129.7 38.4 all-reduce.10
  171.4 62.2 reduce-scatter.28
  237.3 61.3 reduce-scatter.26
  302.6 68.7 reduce-scatter.20
  374.7 61.3 reduce-scatter.22
  440.1 68.5 reduce-scatter.18
  512.0 62.4 reduce-scatter.24
  578.5 66.0 reduce-scatter.16
  646.8 59.7 all-gather.4
